TPU v7x, 32 devices: a whole 2x2x4 slice. The times are simulated.
32 devices in a mesh: gx: 8 (over z, y), gy: 4 (over x, core).
Axes of the slice: x: 2, y: 2, z: 4, core: 2. Of those that a mesh axis runs over, the one named last changes fastest.
Arguments:
- output_one: bfloat16 [300, 12, 1024], P(None, 'gy', 'gx'), may hold values from -6 to 6
- output_two: bfloat16 [300, 12, 1024], P(None, 'gy', 'gx'), may hold values from -6 to 6
- cotan_one: bfloat16 [300, 12, 1024], P(None, 'gy', 'gx'), may hold values from -6 to 6
- cotan_two: bfloat16 [300, 12, 1024], P(None, 'gy', 'gx'), may hold values from -6 to 6
- wet_list: int32 [4, 8, 8, 48], P('gy', 'gx'), may hold values from -1 to 383, as said below
- depth_kernel: bfloat16 [300, 7, 7], replicated, may hold values from -0.875 to 0.875
- expand_weight: bfloat16 [300, 1200], replicated, may hold values from -0.375 to 0.375
- reduce_weight: bfloat16 [1200, 300], replicated, may hold values from -0.1875 to 0.1875
- level_expand: bfloat16 [4, 75, 300], replicated, may hold values from -0.75 to 0.75
- level_reduce: bfloat16 [4, 300, 75], replicated, may hold values from -0.375 to 0.375
Outputs:
- input_one: bfloat16 [300, 12, 1024], P(None, 'gy', 'gx')
- input_two: bfloat16 [300, 12, 1024], P(None, 'gy', 'gx')
- grad_input_one: bfloat16 [300, 12, 1024], P(None, 'gy', 'gx')
- grad_input_two: bfloat16 [300, 12, 1024], P(None, 'gy', 'gx')
- grad_kernel: float32 [300, 7, 7], replicated
- grad_expand: float32 [300, 1200], replicated
- grad_reduce: float32 [1200, 300], replicated
- grad_level_expand: float32 [4, 75, 300], replicated
- grad_level_reduce: float32 [4, 300, 75], replicated
Inputs may be any that keep to these rules, and one draw needn't show every extreme that they name: wet_list[j, i, p, s] is -1 or a cell index row * 128 + column inside the tile at gy index j and gx index i, listed for owner p of the same latitude row of tiles; the indices listed by one tile are distinct and are exactly its wet cells; a tile lists at most 48 cells for one owner, and one owner is listed at most 216 cells by all tiles of its row together.
All inputs are finite; a program needn't handle non-finite values.
Results may differ from a plain program's by a relative error of at most 0.0078.
Values may be sent and summed in bfloat16 or wider, within the bound.
A program may use at most 128 MiB of HBM per device.

v0:
```python
import math
import jax
import jax.numpy as jnp
from jax import lax
from jax.sharding import PartitionSpec as P

EPSILON = 1e-06


def with_halo(shard, sides, width):
    for axis, dim in sides:
        devices, length = (lax.axis_size(axis), shard.shape[dim])
        up = [(i, (i + 1) % devices) for i in range(devices)]
        down = [(j, i) for i, j in up]
        last = lax.slice_in_dim(shard, length - width, length, axis=dim)
        first = lax.slice_in_dim(shard, 0, width, axis=dim)
        before = lax.ppermute(last, axis, up)
        after = lax.ppermute(first, axis, down)
        shard = jnp.concatenate([before, shard, after], axis=dim)
    return shard


def swapped(shard, axis, stride):
    return lax.ppermute(shard, axis, [(i, i ^ 1 << stride) for i in range(lax.axis_size(axis))])


def gelu_slope(argument):
    normal_cdf = 0.5 * (1.0 + lax.erf(argument * 0.7071067811865476))
    return normal_cdf + argument * jnp.exp(-0.5 * argument * argument) * 0.3989422804014327


def level_branch(first_in, second, cot_first, cot_second, cell_mask, level_expand, level_reduce):
    groups, levels, expand_width = level_expand.shape
    column_count = first_in.shape[1]
    grouped = first_in.reshape(groups, levels, column_count)
    level_pre = jnp.einsum(
        "gls,gle->ges", grouped, level_expand, preferred_element_type=jnp.float32
    )
    active = jax.nn.gelu(level_pre, approximate=False).astype(jnp.bfloat16)
    mixed_out = jnp.einsum("ges,gel->gls", active, level_reduce, preferred_element_type=jnp.float32)
    mixed_out = mixed_out.reshape(groups * levels, column_count) * cell_mask[None, :]
    rebuilt = (second.astype(jnp.float32) - mixed_out).astype(jnp.bfloat16)
    upstream = (cot_second * cell_mask.astype(jnp.bfloat16)[None, :]).reshape(
        groups, levels, column_count
    )
    back_act = jnp.einsum(
        "gls,gel->ges", upstream, level_reduce, preferred_element_type=jnp.float32
    )
    back_pre = (back_act * gelu_slope(level_pre)).astype(jnp.bfloat16)
    back_in = jnp.einsum("ges,gle->gls", back_pre, level_expand, preferred_element_type=jnp.float32)
    total_one = (
        cot_first.astype(jnp.float32) + back_in.reshape(groups * levels, column_count)
    ).astype(jnp.bfloat16)
    grad_in = jnp.einsum("gls,ges->gle", grouped, back_pre, preferred_element_type=jnp.float32)
    grad_out = jnp.einsum("ges,gls->gel", active, upstream, preferred_element_type=jnp.float32)
    return (rebuilt, total_one, grad_in, grad_out)


def padded_rims(field_in):
    extended = with_halo(field_in, (("gx", 2), ("gy", 1)), 3)
    tile_rows = field_in.shape[1]
    at_south = lax.axis_index("gy") == 0
    at_north = lax.axis_index("gy") == lax.axis_size("gy") - 1
    row_ids = lax.broadcasted_iota(jnp.int32, (1, extended.shape[1], 1), 1)
    cut_rows = at_south & (row_ids < 3) | at_north & (row_ids >= tile_rows + 3)
    return jnp.where(cut_rows, jnp.zeros_like(extended), extended)


def mirrored(rim_rows):
    for bit_index in range(lax.axis_size("gx").bit_length() - 1):
        rim_rows = swapped(rim_rows, "gx", bit_index)
    return rim_rows


def folded_rims(field_in):
    tile_rows = field_in.shape[1]
    extended = padded_rims(field_in)
    partner = mirrored(extended[:, tile_rows : tile_rows + 3, :])
    upper_rows = partner[:, ::-1, ::-1]
    at_north = lax.axis_index("gy") == lax.axis_size("gy") - 1
    upper_rows = jnp.where(at_north, upper_rows, extended[:, tile_rows + 3 :, :])
    return jnp.concatenate([extended[:, : tile_rows + 3, :], upper_rows], axis=1)


def body(
    output_one,
    output_two,
    cotan_one,
    cotan_two,
    wet_list,
    depth_kernel,
    expand_weight,
    reduce_weight,
    level_expand,
    level_reduce,
):
    channels, tile_rows, tile_cols = output_one.shape
    tile_cells = tile_rows * tile_cols
    flat_one = output_one.reshape(channels, tile_cells)
    flat_two = output_two.reshape(channels, tile_cells)
    flat_cot_one = cotan_one.reshape(channels, tile_cells)
    flat_cot_two = cotan_two.reshape(channels, tile_cells)
    owner_count = wet_list.shape[2]
    slot_count = wet_list.shape[3]
    listing = wet_list.reshape(owner_count, slot_count)
    present = listing >= 0
    cell_index = jnp.where(present, listing, tile_cells).reshape(-1)
    wet_mask = jnp.zeros((tile_cells,), jnp.float32).at[cell_index].set(1.0, mode="drop")
    two_flat, total_flat, grad_level_in, grad_level_out = level_branch(
        flat_one, flat_two, flat_cot_one, flat_cot_two, wet_mask, level_expand, level_reduce
    )
    input_two = two_flat.reshape(channels, tile_rows, tile_cols)
    padded = folded_rims(input_two)
    wide_field = padded.astype(jnp.float32)
    kernel_wide = depth_kernel.astype(jnp.float32)
    spread = jnp.zeros((channels, tile_rows, tile_cols), jnp.float32)
    for row_tap in range(7):
        for col_tap in range(7):
            spread = (
                spread
                + kernel_wide[:, row_tap, col_tap][:, None, None]
                * wide_field[:, row_tap : row_tap + tile_rows, col_tap : col_tap + tile_cols]
            )
    spread = spread.reshape(channels, tile_cells)
    center = spread - jnp.mean(spread, axis=0, keepdims=True)
    rescale = lax.rsqrt(jnp.mean(center * center, axis=0, keepdims=True) + EPSILON)
    normal = center * rescale
    normal_half = normal.astype(jnp.bfloat16)
    contract_first = (((0,), (0,)), ((), ()))
    contract_last = (((1,), (1,)), ((), ()))
    contract_inner = (((1,), (0,)), ((), ()))
    hidden_pre = lax.dot_general(
        expand_weight, normal_half, contract_first, preferred_element_type=jnp.float32
    )
    hidden = jax.nn.gelu(hidden_pre, approximate=False).astype(jnp.bfloat16)
    update = lax.dot_general(
        reduce_weight, hidden, contract_first, preferred_element_type=jnp.float32
    )
    input_one = (flat_one.astype(jnp.float32) - update * wet_mask[None, :]).astype(jnp.bfloat16)
    upstream = total_flat * wet_mask.astype(jnp.bfloat16)[None, :]
    grad_reduce = lax.dot_general(
        hidden, upstream, contract_last, preferred_element_type=jnp.float32
    )
    back_hidden = lax.dot_general(
        reduce_weight, upstream, contract_inner, preferred_element_type=jnp.float32
    )
    back_pre = (back_hidden * gelu_slope(hidden_pre)).astype(jnp.bfloat16)
    grad_expand = lax.dot_general(
        normal_half, back_pre, contract_last, preferred_element_type=jnp.float32
    )
    back_normal = lax.dot_general(
        expand_weight, back_pre, contract_inner, preferred_element_type=jnp.float32
    )
    mean_back = jnp.mean(back_normal, axis=0, keepdims=True)
    mean_cross = jnp.mean(back_normal * normal, axis=0, keepdims=True)
    back_spread = (rescale * (back_normal - mean_back - normal * mean_cross)).astype(jnp.bfloat16)
    back_spread = back_spread.reshape(channels, tile_rows, tile_cols)
    back_field = back_spread.astype(jnp.float32)
    tap_rows = []
    for row_tap in range(7):
        tap_cols = []
        for col_tap in range(7):
            tap_cols.append(
                jnp.sum(
                    back_field
                    * wide_field[:, row_tap : row_tap + tile_rows, col_tap : col_tap + tile_cols],
                    axis=(1, 2),
                )
            )
        tap_rows.append(jnp.stack(tap_cols, axis=1))
    grad_kernel = jnp.stack(tap_rows, axis=1)
    back_padded = padded_rims(back_spread)
    back_wide = back_padded.astype(jnp.float32)
    main_part = jnp.zeros((channels, tile_rows, tile_cols), jnp.float32)
    for row_tap in range(7):
        for col_tap in range(7):
            main_part = (
                main_part
                + kernel_wide[:, row_tap, col_tap][:, None, None]
                * back_wide[
                    :, 6 - row_tap : 6 - row_tap + tile_rows, 6 - col_tap : 6 - col_tap + tile_cols
                ]
            )
    partner = mirrored(back_padded[:, tile_rows : tile_rows + 3, :])
    turned = partner[:, :, ::-1].astype(jnp.float32)
    pieces = []
    for fold_step in (3, 2, 1):
        row_total = jnp.zeros((channels, tile_cols), jnp.float32)
        for row_tap in range(3 + fold_step, min(6, 5 + fold_step) + 1):
            source_row = 5 + fold_step - row_tap
            for col_tap in range(7):
                row_total = (
                    row_total
                    + kernel_wide[:, row_tap, col_tap][:, None]
                    * turned[:, source_row, col_tap : col_tap + tile_cols]
                )
        pieces.append(row_total)
    fold_part = jnp.stack(pieces, axis=1)
    at_north = lax.axis_index("gy") == lax.axis_size("gy") - 1
    fold_part = jnp.where(at_north, fold_part, jnp.zeros_like(fold_part))
    through = main_part.at[:, tile_rows - 3 :, :].add(fold_part)
    grad_input_two = (cotan_two.astype(jnp.float32) + through).astype(jnp.bfloat16)
    summed = lax.psum(
        (grad_kernel, grad_expand, grad_reduce, grad_level_in, grad_level_out), ("gx", "gy")
    )
    factor = 1.0 / math.sqrt(tile_cells * lax.axis_size("gx") * lax.axis_size("gy"))
    return (
        input_one.reshape(channels, tile_rows, tile_cols),
        input_two,
        total_flat.reshape(channels, tile_rows, tile_cols),
        grad_input_two,
        summed[0] * factor,
        summed[1] * factor,
        summed[2] * factor,
        summed[3] * factor,
        summed[4] * factor,
    )


def solution(mesh):
    placed = (
        P(None, "gy", "gx"),
        P(None, "gy", "gx"),
        P(None, "gy", "gx"),
        P(None, "gy", "gx"),
        P("gy", "gx", None, None),
        P(),
        P(),
        P(),
        P(),
        P(),
    )
    return jax.shard_map(
        body,
        mesh=mesh,
        in_specs=placed,
        out_specs=(
            P(None, "gy", "gx"),
            P(None, "gy", "gx"),
            P(None, "gy", "gx"),
            P(None, "gy", "gx"),
            P(),
            P(),
            P(),
            P(),
            P(),
        ),
        check_vma=False,
    )
```

profile of v0, /device:TPU:0, one launch (start us, length us, event | category | flops | bytes accessed | tf_op | source)
XLA Modules:
  0.0 472.8 jit_solution(17439408598463731734)
XLA Ops:
  9.4 2.0 fusion.139
  11.4 4.2 fusion.4
  17.2 2.9 scatter_custom_fusion
  21.4 3.0 collective-permute-start
  24.4 3.0 collective-permute-start.1
  27.9 2.3 fusion.10
  33.5 4.3 collective-permute-done
  37.8 2.2 collective-permute-done.1
  40.0 1.8 pad_maximum_fusion
  50.6 2.1 copy.89
  52.9 2.1 copy.88
  55.1 4.5 maximum_select_fusion
  60.8 2.1 copy.90
  63.2 2.6 fusion.147
  65.8 6.4 %collective-permute-done.4 = bf16[300,3,134]{0,2,1:T(8,128)(2,1)S(1)} collective-permute-done((bf16[300,3,134]{0,2,1:T(8,128)(2,1)}, bf16[300,3,134]{0,2,1:T(8,128)(2,1)S(1)}, u32[]{:S(2)}, u32[]{:S(2)}) %collective-permute-start.4) | collective-permute-done | bytes 241232 | tf_op jit(solution)/shard_map/ppermute | solution.py:24
  72.2 2.7 collective-permute-start.5
  76.2 6.3 %collective-permute-done.5 = bf16[300,3,134]{0,2,1:T(8,128)(2,1)S(1)} collective-permute-done((bf16[300,3,134]{0,2,1:T(8,128)(2,1)S(1)}, bf16[300,3,134]{0,2,1:T(8,128)(2,1)S(1)}, u32[]{:S(2)}, u32[]{:S(2)}) %collective-permute-start.5) | collective-permute-done | bytes 241232 | tf_op jit(solution)/shard_map/ppermute | solution.py:24
  82.5 2.0 collective-permute-start.6
  86.4 12.0 %collective-permute-done.6 = bf16[300,3,134]{0,2,1:T(8,128)(2,1)} collective-permute-done((bf16[300,3,134]{0,2,1:T(8,128)(2,1)S(1)}, bf16[300,3,134]{0,2,1:T(8,128)(2,1)}, u32[]{:S(2)}, u32[]{:S(2)}) %collective-permute-start.6) | collective-permute-done | bytes 241232 | tf_op jit(solution)/shard_map/ppermute | solution.py:24
  98.4 2.1 copy.91
  100.6 5.4 %reverse = bf16[300,3,256]{2,1,0:T(4,128)(2,1)} reverse(bf16[300,3,256]{2,1,0:T(4,128)(2,1)} %bitcast.91), dimensions={1,2} | reverse | bytes 921600
  105.9 2.1 slice_select_fusion
  109.8 36.7 %fusion.167 = (f32[3,128]{1,0:T(4,128)S(1)}, f32[300,3,128]{2,1,0:T(4,128)S(1)}) fusion(f32[300,9,134]{2,1,0:T(8,128)S(1)} %maximum_convert_fusion, f32[300]{0:T(512)S(1)} %get-tuple-element.117, f32[300]{0:T(512)S(1)} %get-tuple-element.118, f32[300]{0:T(512)S(1)} %get-tuple-element.119, f32[300]{0:T(512)S(1)} %copy-done.35, f32[300]{0:T(512)S(1)} %copy-done.37, ...), kind=kLoop, calls=%fused_computation.387 | loop fusion | flops 11289216 | bytes 23100336 | tf_op jit(solution)/shard_map/reduce_sum | solution.py:125
  147.1 4.4 fusion.19
  154.3 31.5 %fusion.80 = (f32[300]{0:T(512)S(1)}, f32[300]{0:T(512)S(1)}, f32[300]{0:T(512)S(1)}, f32[300]{0:T(512)S(1)}, f32[300]{0:T(512)S(1)}, /*index=5*/f32[300]{0:T(51...) fusion(bf16[300,3,128]{2,1,0:T(4,128)(2,1)S(1)} %reshape.526, ...), kind=kLoop, calls=%fused_computation.165 | loop fusion | flops 3106500 | bytes 6236400 | tf_op jit(solution)/shard_map/reduce_sum | solution.py:164
  185.9 34.6 %fusion.82 = (f32[300]{0:T(512)S(1)}, f32[300]{0:T(512)S(1)}, f32[300]{0:T(512)S(1)}, f32[300]{0:T(512)S(1)}, f32[300]{0:T(512)S(1)}, /*index=5*/f32[300]{0:T(51...) fusion(bf16[300,3,128]{2,1,0:T(4,128)(2,1)S(1)} %reshape.526, ...), kind=kLoop, calls=%fused_computation.167 | loop fusion | flops 4257000 | bytes 8546400 | tf_op jit(solution)/shard_map/reduce_sum | solution.py:164
  220.4 35.5 %fusion.81 = (f32[300]{0:T(512)S(1)}, f32[300]{0:T(512)S(1)}, f32[300]{0:T(512)S(1)}, f32[300]{0:T(512)S(1)}, f32[300]{0:T(512)S(1)}, /*index=5*/f32[300]{0:T(51...) fusion(bf16[300,3,128]{2,1,0:T(4,128)(2,1)S(1)} %reshape.526, ...), kind=kLoop, calls=%fused_computation.166 | loop fusion | flops 4257000 | bytes 8546400 | tf_op jit(solution)/shard_map/reduce_sum | solution.py:164
  256.0 1.8 fusion.159
  258.7 1.7 fusion.170
  261.1 1.6 collective-permute-start.7
  262.7 3.4 collective-permute-start.8
  266.3 9.1 %collective-permute-done.7 = bf16[300,3,3]{2,1,0:T(4,128)(2,1)S(1)} collective-permute-done((bf16[300,3,3]{2,1,0:T(4,128)(2,1)}, bf16[300,3,3]{2,1,0:T(4,128)(2,1)S(1)}, u32[]{:S(2)}, u32[]{:S(2)}) %collective-permute-start.7) | collective-permute-done | bytes 5432 | tf_op jit(solution)/shard_map/ppermute | solution.py:17
  275.4 2.1 collective-permute-done.8
  279.7 6.6 %collective-permute-done.10 = bf16[300,3,134]{0,2,1:T(8,128)(2,1)S(1)} collective-permute-done((bf16[300,3,134]{0,2,1:T(8,128)(2,1)S(1)}, bf16[300,3,134]{0,2,1:T(8,128)(2,1)S(1)}, u32[]{:S(2)}, u32[]{:S(2)}) %collective-permute-start.10) | collective-permute-done | bytes 241232 | tf_op jit(solution)/shard_map/ppermute | solution.py:18
  286.7 2.4 collective-permute-done.9
  289.6 4.8 %fusion.166 = (f32[300,9,134]{2,1,0:T(8,128)}, bf16[300,9,134]{2,1,0:T(8,128)(2,1)S(1)}) fusion(bf16[300,3,134]{2,1,0:T(4,128)(2,1)S(1)} %copy.100, bf16[300,3,3]{2,1,0:T(4,128)(2,1)S(1)} %collective-permute-done.8, bf16[300,3,128]{2,1,0:T(4,128)(2,1)S(1)} %reshape.526, bf16[300,3,3]{2,1,0:T(4,128)(2,1)S(1)} %collective-permute-done.7, ...), kind=kLoop, calls=%fused_computation.386 | loop fusion | flops 4341600 | bytes 2894409 | tf_op jit(solution)/shard_map/convert_element_type | solution.py:173
  295.4 9.6 %collective-permute-done.11 = bf16[300,3,134]{0,2,1:T(8,128)(2,1)S(1)} collective-permute-done((bf16[300,3,134]{0,2,1:T(8,128)(2,1)S(1)}, bf16[300,3,134]{0,2,1:T(8,128)(2,1)S(1)}, u32[]{:S(2)}, u32[]{:S(2)}) %collective-permute-start.11) | collective-permute-done | bytes 241232 | tf_op jit(solution)/shard_map/ppermute | solution.py:24
  306.3 9.0 %collective-permute-done.12 = bf16[300,3,134]{0,2,1:T(8,128)(2,1)S(1)} collective-permute-done((bf16[300,3,134]{0,2,1:T(8,128)(2,1)S(1)}, bf16[300,3,134]{0,2,1:T(8,128)(2,1)S(1)}, u32[]{:S(2)}, u32[]{:S(2)}) %collective-permute-start.12) | collective-permute-done | bytes 241232 | tf_op jit(solution)/shard_map/ppermute | solution.py:24
  315.3 2.3 collective-permute-start.13
  317.6 41.8 %psum.35 = f32[300,7,7]{0,2,1:T(8,128)S(1)} all-reduce(f32[300,7,7]{0,2,1:T(8,128)S(1)} %constant_dynamic-update-slice_fusion), channel_id=1, replica_groups=mesh['gx'=8,'gy'=4] {'gx','gy'}, use_global_device_ids=true, to_apply=%region_54.55 | all-reduce | flops 14700 | bytes 117600 | tf_op jit(solution)/shard_map/psum | solution.py:203
  360.7 3.1 reverse.1
  364.5 14.1 %fusion.150 = f32[300,1,128]{2,1,0:T(1,128)S(1)} fusion(f32[300,3,134]{2,1,0:T(4,128)S(1)} %slice_convert_fusion, f32[300]{0:T(512)S(1)} %copy-done.65, f32[300]{0:T(512)S(1)} %copy-done.67, f32[300]{0:T(512)S(1)} %copy-done.69, f32[300]{0:T(512)S(1)} %copy-done.71, f32[300]{0:T(512)S(1)} %copy-done.59, f32[300]{0:T(512)S(1)} %copy-done.61, ...), kind=kLoop, calls=%fused_computation.300 | loop fusion | flops 1574400 | bytes 3404400 | tf_op jit(solution)/shard_map/add | solution.py:193
  378.8 9.3 %multiply_add_fusion.1 = f32[300,1,128]{2,1,0:T(1,128)S(1)} fusion(f32[300,3,134]{2,1,0:T(4,128)S(1)} %slice_convert_fusion, f32[300]{0:T(512)S(1)} %copy-done.44, f32[300]{0:T(512)S(1)} %copy-done.46, f32[300]{0:T(512)S(1)} %copy-done.48, f32[300]{0:T(512)S(1)} %copy-done.50, f32[300]{0:T(512)S(1)} %copy-done.52, f32[300]{0:T(512)S(1)} %copy-done.54, ...), kind=kLoop, calls=%fused_computation.313 | loop fusion | flops 1036800 | bytes 2320800 | tf_op jit(solution)/shard_map/add | solution.py:193
  388.1 4.6 multiply_add_fusion.2
  392.9 37.2 %fusion.86 = bf16[300,3,128]{2,1,0:T(4,128)(2,1)S(1)} fusion(f32[300,9,134]{2,1,0:T(8,128)S(1)} %bitcast.83, f32[300,1,128]{2,1,0:T(1,128)S(1)} %fusion.150, f32[300,1,128]{2,1,0:T(1,128)S(1)} %multiply_add_fusion.1, f32[300,1,128]{2,1,0:T(1,128)S(1)} %multiply_add_fusion.2, f32[300]{0:T(512)S(1)} %copy-done.30, f32[300]{0:T(512)S(1)} %copy-done.32, ...), kind=kLoop, calls=%fused_computation.172 | loop fusion | flops 11980800 | bytes 23559600 | tf_op jit(solution)/shard_map/convert_element_type | solution.py:202
  430.8 28.6 %all-reduce.3.cloned.1.call-done = (f32[300,1200]{1,0:T(8,128)}, f32[1200,300]{0,1:T(8,128)}, f32[4,75,300]{2,1,0:T(8,128)}, f32[4,300,75]{1,2,0:T(8,128)}) async-done(((f32[300,1200]{1,0:T(8,128)}, f32[1200,300]{0,1:T(8,128)}, f32[4,75,300]{2,1,0:T(8,128)}, f32[4,300,75]{1,2,0:T(8,128)}), (f32[300,1200]{1,0:T(8,128)}, f32[1200,300]{0,1:T(8,128)}, f32[4,75,300]{2,1,0:T(8,128)}, ...) | async-done | bytes 3600016 | tf_op jit(solution)/shard_map/psum | solution.py:203
  459.5 2.8 broadcast_multiply_fusion.1
  464.2 1.3 broadcast_multiply_fusion
  (379 shorter events, 37.6 us)
Async XLA Ops:
  7.2 139.9 %copy-start = (bf16[300,1200]{1,0:T(8,128)(2,1)S(1)}, bf16[300,1200]{1,0:T(8,128)(2,1)}, u32[]{:S(2)}) copy-start(bf16[300,1200]{1,0:T(8,128)(2,1)} %param.20) | copy-start | bytes 2160004
  7.2 452.3 %all-reduce.3.cloned.1.call-start = ((), (), s32[]{:S(2)}) async-start(), calls=%async_computation | async-start | bytes 8192000 | tf_op jit(solution)/shard_map/psum | solution.py:203
  16.9 10.5 %copy-start.16 = (bf16[300,3,128]{2,0,1:T(8,128)(2,1)S(1)}, bf16[300,3,128]{2,0,1:T(8,128)(2,1)}, u32[]{:S(2)}) copy-start(bf16[300,3,128]{2,0,1:T(8,128)(2,1)} %param.17) | copy-start | bytes 691204
  17.1 10.6 %copy-start.18 = (bf16[300,3,128]{2,0,1:T(8,128)(2,1)S(1)}, bf16[300,3,128]{2,0,1:T(8,128)(2,1)}, u32[]{:S(2)}) copy-start(bf16[300,3,128]{2,0,1:T(8,128)(2,1)} %param.16) | copy-start | bytes 691204
  21.4 16.4 %collective-permute-start = (bf16[300,3,3]{2,1,0:T(4,128)(2,1)}, bf16[300,3,3]{2,1,0:T(4,128)(2,1)S(1)}, u32[]{:S(2)}, u32[]{:S(2)}) collective-permute-start(bf16[300,3,3]{2,1,0:T(4,128)(2,1)} %get-tuple-element.175), channel_id=1, source_target_pairs={{0,4},{4,8},{8,12},{12,16},{16,20},{20,24},{24,28},{28,0},{1,5},{5... | collective-permute-start | bytes 16208 | tf_op jit(solution)/shard_map/ppermute | solution.py:17
  24.4 15.6 %collective-permute-start.1 = (bf16[300,3,3]{2,1,0:T(4,128)(2,1)}, bf16[300,3,3]{2,1,0:T(4,128)(2,1)}, u32[]{:S(2)}, u32[]{:S(2)}) collective-permute-start(bf16[300,3,3]{2,1,0:T(4,128)(2,1)} %get-tuple-element.176), channel_id=1, source_target_pairs={{4,0},{8,4},{12,8},{16,12},{20,16},{24,20},{28,24},{0,28},{5,1},{9... | collective-permute-start | bytes 16208 | tf_op jit(solution)/shard_map/ppermute | solution.py:18
  42.9 7.8 %collective-permute-start.3 = (bf16[300,3,134]{0,2,1:T(8,128)(2,1)}, bf16[300,3,134]{0,2,1:T(8,128)(2,1)}, u32[]{:S(2)}, u32[]{:S(2)}) collective-permute-start(bf16[300,3,134]{0,2,1:T(8,128)(2,1)} %copy.86), channel_id=1, source_target_pairs={{1,0},{2,1},{3,2},{0,3},{5,4},{6,5},{7,6},{4,7},{9,8},{10,9},{11,1... | collective-permute-start | bytes 723608 | tf_op jit(solution)/shard_map/ppermute | solution.py:18
  42.9 10.1 %collective-permute-start.2 = (bf16[300,3,134]{0,2,1:T(8,128)(2,1)}, bf16[300,3,134]{0,2,1:T(8,128)(2,1)}, u32[]{:S(2)}, u32[]{:S(2)}) collective-permute-start(bf16[300,3,134]{0,2,1:T(8,128)(2,1)} %copy.86), channel_id=1, source_target_pairs={{0,1},{1,2},{2,3},{3,0},{4,5},{5,6},{6,7},{7,4},{8,9},{9,10},{10,1... | collective-permute-start | bytes 723608 | tf_op jit(solution)/shard_map/ppermute | solution.py:17
  50.6 58.8 %copy-start.29 = (f32[300]{0:T(512)}, f32[300]{0:T(512)S(1)}, u32[]{:S(2)}) copy-start(f32[300]{0:T(512)S(1)} %get-tuple-element.117) | copy-start | bytes 3604
  50.6 58.8 %copy-start.31 = (f32[300]{0:T(512)}, f32[300]{0:T(512)S(1)}, u32[]{:S(2)}) copy-start(f32[300]{0:T(512)S(1)} %get-tuple-element.118) | copy-start | bytes 3604
  50.6 58.8 %copy-start.33 = (f32[300]{0:T(512)}, f32[300]{0:T(512)S(1)}, u32[]{:S(2)}) copy-start(f32[300]{0:T(512)S(1)} %get-tuple-element.119) | copy-start | bytes 3604
  59.6 15.3 %copy-start.14 = (bf16[4,75,384]{2,1,0:T(8,128)(2,1)S(1)}, bf16[4,75,384]{2,1,0:T(8,128)(2,1)}, u32[]{:S(2)}) copy-start(bf16[4,75,384]{2,1,0:T(8,128)(2,1)} %copy-done.13) | copy-start | bytes 691204
  62.9 12.1 %copy-start.6 = (bf16[4,300,384]{2,1,0:T(8,128)(2,1)S(1)}, bf16[4,300,384]{2,1,0:T(8,128)(2,1)}, u32[]{:S(2)}) copy-start(bf16[4,300,384]{2,1,0:T(8,128)(2,1)} %copy-done.5) | copy-start | bytes 2764804
  62.9 21.7 %copy-start.8 = (f32[300,384]{1,0:T(8,128)S(1)}, f32[300,384]{1,0:T(8,128)}, u32[]{:S(2)}) copy-start(f32[300,384]{1,0:T(8,128)} %reshape.525) | copy-start | bytes 1382404
  62.9 21.7 %copy-start.9 = (f32[38,8,3,128]{3,1,2,0:T(8,128)S(1)}, f32[38,8,3,128]{3,1,2,0:T(8,128)}, u32[]{:S(2)}) copy-start(f32[38,8,3,128]{3,1,2,0:T(8,128)} %copy.111) | copy-start | bytes 1400836
  62.9 9.4 %collective-permute-start.4 = (bf16[300,3,134]{0,2,1:T(8,128)(2,1)}, bf16[300,3,134]{0,2,1:T(8,128)(2,1)S(1)}, u32[]{:S(2)}, u32[]{:S(2)}) collective-permute-start(bf16[300,3,134]{0,2,1:T(8,128)(2,1)} %copy.90), channel_id=1, source_target_pairs={{0,4},{4,0},{8,12},{12,8},{16,20},{20,16},{24,28},{28,24},{1,5},{5... | collective-permute-start | bytes 723608 | tf_op jit(solution)/shard_map/ppermute | solution.py:24
  72.2 10.3 %collective-permute-start.5 = (bf16[300,3,134]{0,2,1:T(8,128)(2,1)S(1)}, bf16[300,3,134]{0,2,1:T(8,128)(2,1)S(1)}, u32[]{:S(2)}, u32[]{:S(2)}) collective-permute-start(bf16[300,3,134]{0,2,1:T(8,128)(2,1)S(1)} %collective-permute-done.4), channel_id=1, source_target_pairs={{0,8},{4,12},{8,0},{12,4},{16,24},{20,28},{24,16},{28,20},{1,9},{5... | collective-permute-start | bytes 723608 | tf_op jit(solution)/shard_map/ppermute | solution.py:24
  82.5 15.9 %collective-permute-start.6 = (bf16[300,3,134]{0,2,1:T(8,128)(2,1)S(1)}, bf16[300,3,134]{0,2,1:T(8,128)(2,1)}, u32[]{:S(2)}, u32[]{:S(2)}) collective-permute-start(bf16[300,3,134]{0,2,1:T(8,128)(2,1)S(1)} %collective-permute-done.5), channel_id=1, source_target_pairs={{0,16},{4,20},{8,24},{12,28},{16,0},{20,4},{24,8},{28,12},{1,17},{... | collective-permute-start | bytes 723608 | tf_op jit(solution)/shard_map/ppermute | solution.py:24
  109.4 37.2 %copy-start.2 = (f32[300,9,134]{2,1,0:T(8,128)}, f32[300,9,134]{2,1,0:T(8,128)S(1)}, u32[]{:S(2)}) copy-start(f32[300,9,134]{2,1,0:T(8,128)S(1)} %maximum_convert_fusion) | copy-start | bytes 4341604
  220.4 35.5 %copy-start.75 = (f32[384]{0:T(512)S(1)}, f32[384]{0:T(512)}, u32[]{:S(2)}) copy-start(f32[384]{0:T(512)} %copy-done.74) | copy-start | bytes 4612
  220.4 35.5 %copy-start.77 = (f32[384]{0:T(512)S(1)}, f32[384]{0:T(512)}, u32[]{:S(2)}) copy-start(f32[384]{0:T(512)} %copy-done.76) | copy-start | bytes 4612
  261.1 14.3 %collective-permute-start.7 = (bf16[300,3,3]{2,1,0:T(4,128)(2,1)}, bf16[300,3,3]{2,1,0:T(4,128)(2,1)S(1)}, u32[]{:S(2)}, u32[]{:S(2)}) collective-permute-start(bf16[300,3,3]{2,1,0:T(4,128)(2,1)} %get-tuple-element.173), channel_id=1, source_target_pairs={{0,4},{4,8},{8,12},{12,16},{16,20},{20,24},{24,28},{28,0},{1,5},{5... | collective-permute-start | bytes 16208 | tf_op jit(solution)/shard_map/ppermute | solution.py:17
  262.7 14.8 %collective-permute-start.8 = (bf16[300,3,3]{2,1,0:T(4,128)(2,1)S(1)}, bf16[300,3,3]{2,1,0:T(4,128)(2,1)S(1)}, u32[]{:S(2)}, u32[]{:S(2)}) collective-permute-start(bf16[300,3,3]{2,1,0:T(4,128)(2,1)S(1)} %get-tuple-element.174), channel_id=1, source_target_pairs={{4,0},{8,4},{12,8},{16,12},{20,16},{24,20},{28,24},{0,28},{5,1},{9... | collective-permute-start | bytes 16208 | tf_op jit(solution)/shard_map/ppermute | solution.py:18
  266.3 23.3 %copy-start.116 = (pred[9]{0:T(512)(128)(4,1)S(1)}, pred[9]{0:T(512)(128)(4,1)}, u32[]{:S(2)}) copy-start(pred[9]{0:T(512)(128)(4,1)} %and_or_fusion) | copy-start | bytes 31
  278.8 7.6 %collective-permute-start.10 = (bf16[300,3,134]{0,2,1:T(8,128)(2,1)S(1)}, bf16[300,3,134]{0,2,1:T(8,128)(2,1)S(1)}, u32[]{:S(2)}, u32[]{:S(2)}) collective-permute-start(bf16[300,3,134]{0,2,1:T(8,128)(2,1)S(1)} %copy.97), channel_id=1, source_target_pairs={{1,0},{2,1},{3,2},{0,3},{5,4},{6,5},{7,6},{4,7},{9,8},{10,9},{11,1... | collective-permute-start | bytes 723608 | tf_op jit(solution)/shard_map/ppermute | solution.py:18
  279.5 9.7 %collective-permute-start.9 = (bf16[300,3,134]{0,2,1:T(8,128)(2,1)S(1)}, bf16[300,3,134]{0,2,1:T(8,128)(2,1)S(1)}, u32[]{:S(2)}, u32[]{:S(2)}) collective-permute-start(bf16[300,3,134]{0,2,1:T(8,128)(2,1)S(1)} %copy.97), channel_id=1, source_target_pairs={{0,1},{1,2},{2,3},{3,0},{4,5},{5,6},{6,7},{7,4},{8,9},{9,10},{10,1... | collective-permute-start | bytes 723608 | tf_op jit(solution)/shard_map/ppermute | solution.py:17
  295.1 9.9 %collective-permute-start.11 = (bf16[300,3,134]{0,2,1:T(8,128)(2,1)S(1)}, bf16[300,3,134]{0,2,1:T(8,128)(2,1)S(1)}, u32[]{:S(2)}, u32[]{:S(2)}) collective-permute-start(bf16[300,3,134]{0,2,1:T(8,128)(2,1)S(1)} %copy.101), channel_id=1, source_target_pairs={{0,4},{4,0},{8,12},{12,8},{16,20},{20,16},{24,28},{28,24},{1,5},{5... | collective-permute-start | bytes 723608 | tf_op jit(solution)/shard_map/ppermute | solution.py:24
  305.0 10.3 %collective-permute-start.12 = (bf16[300,3,134]{0,2,1:T(8,128)(2,1)S(1)}, bf16[300,3,134]{0,2,1:T(8,128)(2,1)S(1)}, u32[]{:S(2)}, u32[]{:S(2)}) collective-permute-start(bf16[300,3,134]{0,2,1:T(8,128)(2,1)S(1)} %collective-permute-done.11), channel_id=1, source_target_pairs={{0,8},{4,12},{8,0},{12,4},{16,24},{20,28},{24,16},{28,20},{1,9},{5... | collective-permute-start | bytes 723608 | tf_op jit(solution)/shard_map/ppermute | solution.py:24
  306.2 86.5 %slice-start = ((s8[4915200]{0:T(1024)(128)(4,1)}), s8[720896]{0:T(1024)(128)(4,1)S(1)}, s32[]{:S(2)}) async-start(s8[4915200]{0:T(1024)(128)(4,1)} %bitcast.82), calls=%async_computation.1 | async-start | bytes 1441792
  315.3 45.0 %collective-permute-start.13 = (bf16[300,3,134]{0,2,1:T(8,128)(2,1)S(1)}, bf16[300,3,134]{0,2,1:T(8,128)(2,1)S(1)}, u32[]{:S(2)}, u32[]{:S(2)}) collective-permute-start(bf16[300,3,134]{0,2,1:T(8,128)(2,1)S(1)} %collective-permute-done.12), channel_id=1, source_target_pairs={{0,16},{4,20},{8,24},{12,28},{16,0},{20,4},{24,8},{28,12},{1,17},{... | collective-permute-start | bytes 723608 | tf_op jit(solution)/shard_map/ppermute | solution.py:24
  363.8 28.9 %slice-start.1 = ((s8[4915200]{0:T(1024)(128)(4,1)}), s8[4194304]{0:T(1024)(128)(4,1)S(1)}, s32[]{:S(2)}) async-start(s8[4915200]{0:T(1024)(128)(4,1)} %bitcast.82), calls=%async_computation.2 | async-start | bytes 8388608
  378.6 14.1 %copy-start.17 = (bf16[300,3,128]{2,0,1:T(8,128)(2,1)S(1)}, bf16[300,3,128]{2,0,1:T(8,128)(2,1)}, u32[]{:S(2)}) copy-start(bf16[300,3,128]{2,0,1:T(8,128)(2,1)} %param.17) | copy-start | bytes 691204
  378.6 14.1 %copy-start.79 = (f32[300]{0:T(512)S(1)}, f32[300]{0:T(512)}, u32[]{:S(2)}) copy-start(f32[300]{0:T(512)} %get-tuple-element.154) | copy-start | bytes 3604
  378.6 14.1 %copy-start.81 = (f32[300]{0:T(512)S(1)}, f32[300]{0:T(512)}, u32[]{:S(2)}) copy-start(f32[300]{0:T(512)} %get-tuple-element.155) | copy-start | bytes 3604
  378.6 14.1 %copy-start.83 = (f32[300]{0:T(512)S(1)}, f32[300]{0:T(512)}, u32[]{:S(2)}) copy-start(f32[300]{0:T(512)} %get-tuple-element.156) | copy-start | bytes 3604
  378.7 14.1 %copy-start.85 = (f32[300]{0:T(512)S(1)}, f32[300]{0:T(512)}, u32[]{:S(2)}) copy-start(f32[300]{0:T(512)} %get-tuple-element.157) | copy-start | bytes 3604
  378.7 14.1 %copy-start.87 = (f32[300]{0:T(512)S(1)}, f32[300]{0:T(512)}, u32[]{:S(2)}) copy-start(f32[300]{0:T(512)} %get-tuple-element.158) | copy-start | bytes 3604
  378.7 14.1 %copy-start.89 = (f32[300]{0:T(512)S(1)}, f32[300]{0:T(512)}, u32[]{:S(2)}) copy-start(f32[300]{0:T(512)} %get-tuple-element.159) | copy-start | bytes 3604
  378.7 14.1 %copy-start.91 = (f32[300]{0:T(512)S(1)}, f32[300]{0:T(512)}, u32[]{:S(2)}) copy-start(f32[300]{0:T(512)} %get-tuple-element.160) | copy-start | bytes 3604
  378.7 14.1 %copy-start.93 = (f32[300]{0:T(512)S(1)}, f32[300]{0:T(512)}, u32[]{:S(2)}) copy-start(f32[300]{0:T(512)} %get-tuple-element.161) | copy-start | bytes 3604
  378.7 14.1 %copy-start.95 = (f32[300]{0:T(512)S(1)}, f32[300]{0:T(512)}, u32[]{:S(2)}) copy-start(f32[300]{0:T(512)} %get-tuple-element.162) | copy-start | bytes 3604
  378.7 14.1 %copy-start.97 = (f32[300]{0:T(512)S(1)}, f32[300]{0:T(512)}, u32[]{:S(2)}) copy-start(f32[300]{0:T(512)} %get-tuple-element.163) | copy-start | bytes 3604
  378.7 14.1 %copy-start.99 = (f32[300]{0:T(512)S(1)}, f32[300]{0:T(512)}, u32[]{:S(2)}) copy-start(f32[300]{0:T(512)} %get-tuple-element.164) | copy-start | bytes 3604
  378.7 14.1 %copy-start.101 = (f32[300]{0:T(512)S(1)}, f32[300]{0:T(512)}, u32[]{:S(2)}) copy-start(f32[300]{0:T(512)} %get-tuple-element.135) | copy-start | bytes 3604
  378.7 14.1 %copy-start.103 = (f32[300]{0:T(512)S(1)}, f32[300]{0:T(512)}, u32[]{:S(2)}) copy-start(f32[300]{0:T(512)} %get-tuple-element.139) | copy-start | bytes 3604
  378.8 14.1 %copy-start.105 = (f32[300]{0:T(512)S(1)}, f32[300]{0:T(512)}, u32[]{:S(2)}) copy-start(f32[300]{0:T(512)} %get-tuple-element.140) | copy-start | bytes 3604
  378.8 14.1 %copy-start.107 = (f32[300]{0:T(512)S(1)}, f32[300]{0:T(512)}, u32[]{:S(2)}) copy-start(f32[300]{0:T(512)} %get-tuple-element.141) | copy-start | bytes 3604
  378.8 14.1 %copy-start.109 = (f32[300]{0:T(512)S(1)}, f32[300]{0:T(512)}, u32[]{:S(2)}) copy-start(f32[300]{0:T(512)} %get-tuple-element.142) | copy-start | bytes 3604
  (86 other events, 250.1 us)
Sparse Core Ops, SparseCore 0:
  306.4 153.0 all-reduce.2
where the time goes:
time: 480 us; the launch traced here: 473 us
  other arithmetic  232 us (48%)
  waiting for transfers between devices  98.9 us (21%)
  local copies, waits for them, and re-layouts  44 us (9%)
  blocking collectives  41.8 us (9%)
  starting transfers between devices  20.4 us (4%)
  matrix products  19.1 us (4%)
  between operations  16.9 us (4%)
    reduce_sum x3, other arithmetic, body(): jnp.sum(back_field * wide_field[:, row_tap:row_tap + tile_rows, col_tap:c...  102 us
    ppermute x6, waiting for transfers between devices, swapped(): lax.ppermute(shard, axis, [(i, i ^ 1 << stride) for i in range(lax.axis_s...  43.3 us
    psum x1, blocking collectives, body(): lax.psum((grad_kernel, grad_expand, grad_reduce, grad_level_in, grad_leve...  41.8 us
    convert_element_type x1, other arithmetic, body(): (cotan_two.astype(jnp.float32) + through).astype(jnp.bfloat16)  37.2 us
    reduce_sum x1, other arithmetic, body(): center = spread - jnp.mean(spread, axis=0, keepdims=True)  36.7 us
    psum x1, waiting for transfers between devices, body(): lax.psum((grad_kernel, grad_expand, grad_reduce, grad_level_in, grad_leve...  28.6 us
    add x3, other arithmetic, body(): row_total + kernel_wide[:, row_tap, col_tap][:, None] * turned[:, source_...  28 us
    unnamed x260, local copies, waits for them, and re-layouts  18.8 us
  transfers between devices with their start and end apart: 15, of which 13 were waited for; matrix products, arithmetic and copies ran while one was open for 19% of the time, Pallas kernels for 0%

commit v1 on v0

--- a/solution.py
+++ b/solution.py
@@ -94,6 +94,12 @@
     level_expand,
     level_reduce,
 ):
+
+    def arrange_levels_all(frame_in, mesh_ax, across):
+        for to_i in (mesh_ax, across):
+            frame_in = lax.psum(frame_in, to_i)
+        return frame_in
+
     channels, tile_rows, tile_cols = output_one.shape
     tile_cells = tile_rows * tile_cols
     flat_one = output_one.reshape(channels, tile_cells)
@@ -200,8 +206,8 @@
     fold_part = jnp.where(at_north, fold_part, jnp.zeros_like(fold_part))
     through = main_part.at[:, tile_rows - 3 :, :].add(fold_part)
     grad_input_two = (cotan_two.astype(jnp.float32) + through).astype(jnp.bfloat16)
-    summed = lax.psum(
-        (grad_kernel, grad_expand, grad_reduce, grad_level_in, grad_level_out), ("gx", "gy")
+    summed = arrange_levels_all(
+        (grad_kernel, grad_expand, grad_reduce, grad_level_in, grad_level_out), "gy", "gx"
     )
     factor = 1.0 / math.sqrt(tile_cells * lax.axis_size("gx") * lax.axis_size("gy"))
     return (

time: 480 us -> 547 us (1.14)
  other arithmetic: 232 us -> 266 us
  waiting for transfers between devices: 98.9 us -> 119 us
  blocking collectives: 41.8 us -> 53.1 us
    convert_element_type x1, other arithmetic: 37.2 us -> 70.2 us  [body(): (cotan_two.astype(jnp.float32) + through).astype(jnp.bfloat16)]
    psum x1 -> x2, waiting for transfers between devices: 28.6 us -> 53.9 us  [arrange_levels_all(): frame_in = lax.psum(frame_in, to_i)]
    psum x1 -> x2, blocking collectives: 41.8 us -> 53.1 us  [arrange_levels_all(): frame_in = lax.psum(frame_in, to_i)]
    ppermute x6, waiting for transfers between devices: 43.3 us -> 32.8 us  [swapped(): lax.ppermute(shard, axis, [(i, i ^ 1 << stride) for i in range(lax.axis_s...]
    ppermute x4, waiting for transfers between devices: 10.9 us -> 18.6 us  [with_halo(): after = lax.ppermute(first, axis, down)]
    unnamed x260 -> x280, local copies, waits for them, and re-layouts: 18.8 us -> 19.5 us
  transfers between devices with their start and end apart: 15 -> 16, of which waited for: 13 -> 12; matrix products, arithmetic and copies ran while one was open for 19% -> 25% of each run, Pallas kernels for 0% -> 0%
where the time goes in v1:
time: 547 us; the launch traced here: 540 us
  other arithmetic  266 us (49%)
  waiting for transfers between devices  119 us (22%)
  blocking collectives  53.1 us (10%)
  local copies, waits for them, and re-layouts  44.9 us (8%)
  starting transfers between devices  21 us (4%)
  matrix products  19.1 us (3%)
  between operations  17 us (3%)
    reduce_sum x3, other arithmetic, body(): jnp.sum(back_field * wide_field[:, row_tap:row_tap + tile_rows, col_tap:c...  102 us
    convert_element_type x1, other arithmetic, body(): (cotan_two.astype(jnp.float32) + through).astype(jnp.bfloat16)  70.2 us
    psum x2, waiting for transfers between devices, arrange_levels_all(): frame_in = lax.psum(frame_in, to_i)  53.9 us
    psum x2, blocking collectives, arrange_levels_all(): frame_in = lax.psum(frame_in, to_i)  53.1 us
    reduce_sum x1, other arithmetic, body(): center = spread - jnp.mean(spread, axis=0, keepdims=True)  36.7 us
    ppermute x6, waiting for transfers between devices, swapped(): lax.ppermute(shard, axis, [(i, i ^ 1 << stride) for i in range(lax.axis_s...  32.8 us
    add x3, other arithmetic, body(): row_total + kernel_wide[:, row_tap, col_tap][:, None] * turned[:, source_...  28 us
    unnamed x280, local copies, waits for them, and re-layouts  19.5 us
  transfers between devices with their start and end apart: 16, of which 12 were waited for; matrix products, arithmetic and copies ran while one was open for 25% of the time, Pallas kernels for 0%

profile of v1, /device:TPU:0, one launch (start us, length us, event | category | flops | bytes accessed | tf_op | source)
XLA Modules:
  0.0 540.2 jit_solution(7123540591526650969)
XLA Ops:
  9.4 2.0 fusion.139
  11.4 4.2 fusion.4
  17.2 2.9 scatter_custom_fusion
  21.4 3.0 collective-permute-start
  24.4 3.0 collective-permute-start.1
  27.9 2.3 fusion.10
  33.4 4.4 collective-permute-done
  37.8 2.2 collective-permute-done.1
  40.0 1.8 pad_maximum_fusion
  50.7 2.1 copy.89
  52.9 2.1 copy.88
  55.1 4.5 maximum_select_fusion
  60.8 2.1 copy.90
  63.2 2.6 fusion.147
  65.8 6.4 %collective-permute-done.4 = bf16[300,3,134]{0,2,1:T(8,128)(2,1)S(1)} collective-permute-done((bf16[300,3,134]{0,2,1:T(8,128)(2,1)}, bf16[300,3,134]{0,2,1:T(8,128)(2,1)S(1)}, u32[]{:S(2)}, u32[]{:S(2)}) %collective-permute-start.4) | collective-permute-done | bytes 241232 | tf_op jit(solution)/shard_map/ppermute | solution.py:24
  72.2 2.7 collective-permute-start.5
  76.2 6.3 %collective-permute-done.5 = bf16[300,3,134]{0,2,1:T(8,128)(2,1)S(1)} collective-permute-done((bf16[300,3,134]{0,2,1:T(8,128)(2,1)S(1)}, bf16[300,3,134]{0,2,1:T(8,128)(2,1)S(1)}, u32[]{:S(2)}, u32[]{:S(2)}) %collective-permute-start.5) | collective-permute-done | bytes 241232 | tf_op jit(solution)/shard_map/ppermute | solution.py:24
  82.5 2.0 collective-permute-start.6
  86.4 12.0 %collective-permute-done.6 = bf16[300,3,134]{0,2,1:T(8,128)(2,1)} collective-permute-done((bf16[300,3,134]{0,2,1:T(8,128)(2,1)S(1)}, bf16[300,3,134]{0,2,1:T(8,128)(2,1)}, u32[]{:S(2)}, u32[]{:S(2)}) %collective-permute-start.6) | collective-permute-done | bytes 241232 | tf_op jit(solution)/shard_map/ppermute | solution.py:24
  98.4 2.1 copy.91
  100.6 5.4 reverse
  105.9 2.1 slice_select_fusion
  109.8 36.7 %fusion.167 = (f32[3,128]{1,0:T(4,128)S(1)}, f32[300,3,128]{2,1,0:T(4,128)S(1)}) fusion(f32[300,9,134]{2,1,0:T(8,128)S(1)} %maximum_convert_fusion, f32[300]{0:T(512)S(1)} %get-tuple-element.117, f32[300]{0:T(512)S(1)} %get-tuple-element.118, f32[300]{0:T(512)S(1)} %get-tuple-element.119, f32[300]{0:T(512)S(1)} %copy-done.35, f32[300]{0:T(512)S(1)} %copy-done.37, ...), kind=kLoop, calls=%fused_computation.387 | loop fusion | flops 11289216 | bytes 23100336 | tf_op jit(solution)/shard_map/reduce_sum | solution.py:131
  147.1 4.4 fusion.19
  154.3 31.5 %fusion.80 = (f32[300]{0:T(512)S(1)}, f32[300]{0:T(512)S(1)}, f32[300]{0:T(512)S(1)}, f32[300]{0:T(512)S(1)}, f32[300]{0:T(512)S(1)}, /*index=5*/f32[300]{0:T(51...) fusion(bf16[300,3,128]{2,1,0:T(4,128)(2,1)S(1)} %reshape.526, ...), kind=kLoop, calls=%fused_computation.165 | loop fusion | flops 3106500 | bytes 6236400 | tf_op jit(solution)/shard_map/reduce_sum | solution.py:170
  185.9 34.6 %fusion.82 = (f32[300]{0:T(512)S(1)}, f32[300]{0:T(512)S(1)}, f32[300]{0:T(512)S(1)}, f32[300]{0:T(512)S(1)}, f32[300]{0:T(512)S(1)}, /*index=5*/f32[300]{0:T(51...) fusion(bf16[300,3,128]{2,1,0:T(4,128)(2,1)S(1)} %reshape.526, ...), kind=kLoop, calls=%fused_computation.167 | loop fusion | flops 4257000 | bytes 8546400 | tf_op jit(solution)/shard_map/reduce_sum | solution.py:170
  220.4 36.0 %fusion.81 = (f32[300]{0:T(512)}, f32[300]{0:T(512)S(1)}, f32[300]{0:T(512)S(1)}, f32[300]{0:T(512)S(1)}, f32[300]{0:T(512)S(1)}, /*index=5*/f32[300]{0:T(512)S(...) fusion(bf16[300,3,128]{2,1,0:T(4,128)(2,1)S(1)} %reshape.526, ...), kind=kLoop, calls=%fused_computation.166 | loop fusion | flops 4257000 | bytes 8546400 | tf_op jit(solution)/shard_map/reduce_sum | solution.py:170
  256.5 1.7 fusion.159
  258.5 1.7 fusion.170
  260.6 1.6 collective-permute-start.7
  262.2 3.2 collective-permute-start.8
  265.9 8.6 %collective-permute-done.7 = bf16[300,3,3]{2,1,0:T(4,128)(2,1)S(1)} collective-permute-done((bf16[300,3,3]{2,1,0:T(4,128)(2,1)S(1)}, bf16[300,3,3]{2,1,0:T(4,128)(2,1)S(1)}, u32[]{:S(2)}, u32[]{:S(2)}) %collective-permute-start.7) | collective-permute-done | bytes 5432 | tf_op jit(solution)/shard_map/ppermute | solution.py:17
  274.6 2.2 collective-permute-done.8
  279.2 14.2 %collective-permute-done.10 = bf16[300,3,134]{0,2,1:T(8,128)(2,1)} collective-permute-done((bf16[300,3,134]{0,2,1:T(8,128)(2,1)S(1)}, bf16[300,3,134]{0,2,1:T(8,128)(2,1)}, u32[]{:S(2)}, u32[]{:S(2)}) %collective-permute-start.10) | collective-permute-done | bytes 241232 | tf_op jit(solution)/shard_map/ppermute | solution.py:18
  293.3 1.3 copy.100
  295.8 5.4 %fusion.166 = (f32[300,9,134]{2,1,0:T(8,128)}, bf16[300,9,134]{2,1,0:T(8,128)(2,1)S(1)}) fusion(bf16[300,3,134]{2,1,0:T(4,128)(2,1)S(1)} %copy.100, bf16[300,3,3]{2,1,0:T(4,128)(2,1)S(1)} %collective-permute-done.8, bf16[300,3,128]{2,1,0:T(4,128)(2,1)S(1)} %reshape.526, bf16[300,3,3]{2,1,0:T(4,128)(2,1)S(1)} %collective-permute-done.7, ...), kind=kLoop, calls=%fused_computation.386 | loop fusion | flops 4341600 | bytes 2894409 | tf_op jit(solution)/shard_map/convert_element_type | solution.py:179
  302.0 14.3 %psum.70 = f32[300,7,7]{0,2,1:T(8,128)S(1)} all-reduce(f32[300,7,7]{0,2,1:T(8,128)S(1)} %constant_dynamic-update-slice_fusion), channel_id=1, replica_groups=mesh['gx'=8,'gy'=4] {'gy'}, use_global_device_ids=true, to_apply=%region_54.55 | all-reduce | flops 14700 | bytes 117600 | tf_op jit(solution)/shard_map/psum | solution.py:100
  318.0 8.0 %collective-permute-done.12 = bf16[300,3,134]{0,2,1:T(8,128)(2,1)S(1)} collective-permute-done((bf16[300,3,134]{0,2,1:T(8,128)(2,1)}, bf16[300,3,134]{0,2,1:T(8,128)(2,1)S(1)}, u32[]{:S(2)}, u32[]{:S(2)}) %collective-permute-start.12) | collective-permute-done | bytes 241232 | tf_op jit(solution)/shard_map/ppermute | solution.py:24
  326.0 2.1 collective-permute-start.13
  328.1 38.8 %psum.71 = f32[300,7,7]{0,2,1:T(8,128)S(1)} all-reduce(f32[300,7,7]{0,2,1:T(8,128)S(1)} %psum.70), channel_id=1, replica_groups=mesh['gx'=8,'gy'=4] {'gx'}, use_global_device_ids=true, to_apply=%region_55.56 | all-reduce | flops 14700 | bytes 117600 | tf_op jit(solution)/shard_map/psum | solution.py:100
  368.8 3.1 reverse.1
  373.2 9.3 %multiply_add_fusion.1 = f32[300,1,128]{2,1,0:T(1,128)S(1)} fusion(f32[300,3,134]{2,1,0:T(4,128)S(1)} %slice_convert_fusion, f32[300]{0:T(512)S(1)} %copy-done.44, f32[300]{0:T(512)S(1)} %copy-done.46, f32[300]{0:T(512)S(1)} %copy-done.48, f32[300]{0:T(512)S(1)} %copy-done.50, f32[300]{0:T(512)S(1)} %copy-done.52, f32[300]{0:T(512)S(1)} %copy-done.54, ...), kind=kLoop, calls=%fused_computation.313 | loop fusion | flops 1036800 | bytes 2320800 | tf_op jit(solution)/shard_map/add | solution.py:199
  382.6 4.6 multiply_add_fusion.2
  387.5 14.1 %fusion.150 = f32[300,1,128]{2,1,0:T(1,128)S(1)} fusion(f32[300,3,134]{2,1,0:T(4,128)S(1)} %slice_convert_fusion, f32[300]{0:T(512)S(1)} %copy-done.65, f32[300]{0:T(512)S(1)} %copy-done.67, f32[300]{0:T(512)S(1)} %copy-done.69, f32[300]{0:T(512)S(1)} %copy-done.71, f32[300]{0:T(512)S(1)} %copy-done.59, f32[300]{0:T(512)S(1)} %copy-done.61, ...), kind=kLoop, calls=%fused_computation.300 | loop fusion | flops 1574400 | bytes 3404400 | tf_op jit(solution)/shard_map/add | solution.py:199
  402.0 70.2 %fusion.86 = bf16[300,3,128]{2,1,0:T(4,128)(2,1)S(1)} fusion(f32[300,9,134]{2,1,0:T(8,128)} %get-tuple-element.173, f32[300,1,128]{2,1,0:T(1,128)S(1)} %fusion.150, f32[300,1,128]{2,1,0:T(1,128)S(1)} %multiply_add_fusion.1, f32[300,1,128]{2,1,0:T(1,128)S(1)} %multiply_add_fusion.2, f32[300]{0:T(512)S(1)} %copy-done.30, f32[300]{0:T(512)S(1)} %copy-done.32, ...), kind=kLoop, calls=%fused_computation.172 | loop fusion | flops 11980800 | bytes 23559600 | tf_op jit(solution)/shard_map/convert_element_type | solution.py:208
  472.9 53.9 %all-reduce.5.cloned.1.call-done = (f32[300,1200]{1,0:T(8,128)}, f32[1200,300]{0,1:T(8,128)}, f32[4,75,300]{2,1,0:T(8,128)}, f32[4,300,75]{1,2,0:T(8,128)}) async-done(((f32[300,1200]{1,0:T(8,128)}, f32[1200,300]{0,1:T(8,128)}, f32[4,75,300]{2,1,0:T(8,128)}, f32[4,300,75]{1,2,0:T(8,128)}), (f32[300,1200]{1,0:T(8,128)}, f32[1200,300]{0,1:T(8,128)}, f32[4,75,300]{2,1,0:T(8,128)}, ...) | async-done | bytes 3600016 | tf_op jit(solution)/shard_map/psum | solution.py:100
  526.8 2.8 broadcast_multiply_fusion.1
  531.5 1.3 broadcast_multiply_fusion
  (402 shorter events, 39.0 us)
Async XLA Ops:
  7.2 139.9 %copy-start = (bf16[300,1200]{1,0:T(8,128)(2,1)S(1)}, bf16[300,1200]{1,0:T(8,128)(2,1)}, u32[]{:S(2)}) copy-start(bf16[300,1200]{1,0:T(8,128)(2,1)} %param.20) | copy-start | bytes 2160004
  7.2 365.2 %all-reduce.7.cloned.1.call-start = ((), (), s32[]{:S(2)}) async-start(), calls=%async_computation.1 | async-start | bytes 8192000 | tf_op jit(solution)/shard_map/psum | solution.py:100
  21.4 16.4 %collective-permute-start = (bf16[300,3,3]{2,1,0:T(4,128)(2,1)}, bf16[300,3,3]{2,1,0:T(4,128)(2,1)S(1)}, u32[]{:S(2)}, u32[]{:S(2)}) collective-permute-start(bf16[300,3,3]{2,1,0:T(4,128)(2,1)} %get-tuple-element.179), channel_id=1, source_target_pairs={{0,4},{4,8},{8,12},{12,16},{16,20},{20,24},{24,28},{28,0},{1,5},{5... | collective-permute-start | bytes 16208 | tf_op jit(solution)/shard_map/ppermute | solution.py:17
  24.4 15.6 %collective-permute-start.1 = (bf16[300,3,3]{2,1,0:T(4,128)(2,1)}, bf16[300,3,3]{2,1,0:T(4,128)(2,1)}, u32[]{:S(2)}, u32[]{:S(2)}) collective-permute-start(bf16[300,3,3]{2,1,0:T(4,128)(2,1)} %get-tuple-element.180), channel_id=1, source_target_pairs={{4,0},{8,4},{12,8},{16,12},{20,16},{24,20},{28,24},{0,28},{5,1},{9... | collective-permute-start | bytes 16208 | tf_op jit(solution)/shard_map/ppermute | solution.py:18
  42.9 7.8 %collective-permute-start.3 = (bf16[300,3,134]{0,2,1:T(8,128)(2,1)}, bf16[300,3,134]{0,2,1:T(8,128)(2,1)}, u32[]{:S(2)}, u32[]{:S(2)}) collective-permute-start(bf16[300,3,134]{0,2,1:T(8,128)(2,1)} %copy.86), channel_id=1, source_target_pairs={{1,0},{2,1},{3,2},{0,3},{5,4},{6,5},{7,6},{4,7},{9,8},{10,9},{11,1... | collective-permute-start | bytes 723608 | tf_op jit(solution)/shard_map/ppermute | solution.py:18
  42.9 10.1 %collective-permute-start.2 = (bf16[300,3,134]{0,2,1:T(8,128)(2,1)}, bf16[300,3,134]{0,2,1:T(8,128)(2,1)}, u32[]{:S(2)}, u32[]{:S(2)}) collective-permute-start(bf16[300,3,134]{0,2,1:T(8,128)(2,1)} %copy.86), channel_id=1, source_target_pairs={{0,1},{1,2},{2,3},{3,0},{4,5},{5,6},{6,7},{7,4},{8,9},{9,10},{10,1... | collective-permute-start | bytes 723608 | tf_op jit(solution)/shard_map/ppermute | solution.py:17
  50.7 58.7 %copy-start.29 = (f32[300]{0:T(512)}, f32[300]{0:T(512)S(1)}, u32[]{:S(2)}) copy-start(f32[300]{0:T(512)S(1)} %get-tuple-element.117) | copy-start | bytes 3604
  50.7 58.7 %copy-start.31 = (f32[300]{0:T(512)}, f32[300]{0:T(512)S(1)}, u32[]{:S(2)}) copy-start(f32[300]{0:T(512)S(1)} %get-tuple-element.118) | copy-start | bytes 3604
  50.7 58.7 %copy-start.33 = (f32[300]{0:T(512)}, f32[300]{0:T(512)S(1)}, u32[]{:S(2)}) copy-start(f32[300]{0:T(512)S(1)} %get-tuple-element.119) | copy-start | bytes 3604
  59.6 15.3 %copy-start.14 = (bf16[4,75,384]{2,1,0:T(8,128)(2,1)S(1)}, bf16[4,75,384]{2,1,0:T(8,128)(2,1)}, u32[]{:S(2)}) copy-start(bf16[4,75,384]{2,1,0:T(8,128)(2,1)} %copy-done.13) | copy-start | bytes 691204
  62.9 21.7 %copy-start.8 = (f32[300,384]{1,0:T(8,128)S(1)}, f32[300,384]{1,0:T(8,128)}, u32[]{:S(2)}) copy-start(f32[300,384]{1,0:T(8,128)} %reshape.525) | copy-start | bytes 1382404
  62.9 21.7 %copy-start.9 = (f32[38,8,3,128]{3,1,2,0:T(8,128)S(1)}, f32[38,8,3,128]{3,1,2,0:T(8,128)}, u32[]{:S(2)}) copy-start(f32[38,8,3,128]{3,1,2,0:T(8,128)} %copy.111) | copy-start | bytes 1400836
  62.9 9.4 %collective-permute-start.4 = (bf16[300,3,134]{0,2,1:T(8,128)(2,1)}, bf16[300,3,134]{0,2,1:T(8,128)(2,1)S(1)}, u32[]{:S(2)}, u32[]{:S(2)}) collective-permute-start(bf16[300,3,134]{0,2,1:T(8,128)(2,1)} %copy.90), channel_id=1, source_target_pairs={{0,4},{4,0},{8,12},{12,8},{16,20},{20,16},{24,28},{28,24},{1,5},{5... | collective-permute-start | bytes 723608 | tf_op jit(solution)/shard_map/ppermute | solution.py:24
  72.2 10.3 %collective-permute-start.5 = (bf16[300,3,134]{0,2,1:T(8,128)(2,1)S(1)}, bf16[300,3,134]{0,2,1:T(8,128)(2,1)S(1)}, u32[]{:S(2)}, u32[]{:S(2)}) collective-permute-start(bf16[300,3,134]{0,2,1:T(8,128)(2,1)S(1)} %collective-permute-done.4), channel_id=1, source_target_pairs={{0,8},{4,12},{8,0},{12,4},{16,24},{20,28},{24,16},{28,20},{1,9},{5... | collective-permute-start | bytes 723608 | tf_op jit(solution)/shard_map/ppermute | solution.py:24
  82.5 15.9 %collective-permute-start.6 = (bf16[300,3,134]{0,2,1:T(8,128)(2,1)S(1)}, bf16[300,3,134]{0,2,1:T(8,128)(2,1)}, u32[]{:S(2)}, u32[]{:S(2)}) collective-permute-start(bf16[300,3,134]{0,2,1:T(8,128)(2,1)S(1)} %collective-permute-done.5), channel_id=1, source_target_pairs={{0,16},{4,20},{8,24},{12,28},{16,0},{20,4},{24,8},{28,12},{1,17},{... | collective-permute-start | bytes 723608 | tf_op jit(solution)/shard_map/ppermute | solution.py:24
  109.4 37.2 %copy-start.2 = (f32[300,9,134]{2,1,0:T(8,128)}, f32[300,9,134]{2,1,0:T(8,128)S(1)}, u32[]{:S(2)}) copy-start(f32[300,9,134]{2,1,0:T(8,128)S(1)} %maximum_convert_fusion) | copy-start | bytes 4341604
  220.4 36.1 %copy-start.75 = (f32[384]{0:T(512)S(1)}, f32[384]{0:T(512)}, u32[]{:S(2)}) copy-start(f32[384]{0:T(512)} %copy-done.74) | copy-start | bytes 4612
  220.4 36.1 %copy-start.77 = (f32[384]{0:T(512)S(1)}, f32[384]{0:T(512)}, u32[]{:S(2)}) copy-start(f32[384]{0:T(512)} %copy-done.76) | copy-start | bytes 4612
  260.6 14.0 %collective-permute-start.7 = (bf16[300,3,3]{2,1,0:T(4,128)(2,1)S(1)}, bf16[300,3,3]{2,1,0:T(4,128)(2,1)S(1)}, u32[]{:S(2)}, u32[]{:S(2)}) collective-permute-start(bf16[300,3,3]{2,1,0:T(4,128)(2,1)S(1)} %get-tuple-element.177), channel_id=1, source_target_pairs={{0,4},{4,8},{8,12},{12,16},{16,20},{20,24},{24,28},{28,0},{1,5},{5... | collective-permute-start | bytes 16208 | tf_op jit(solution)/shard_map/ppermute | solution.py:17
  262.2 14.6 %collective-permute-start.8 = (bf16[300,3,3]{2,1,0:T(4,128)(2,1)S(1)}, bf16[300,3,3]{2,1,0:T(4,128)(2,1)S(1)}, u32[]{:S(2)}, u32[]{:S(2)}) collective-permute-start(bf16[300,3,3]{2,1,0:T(4,128)(2,1)S(1)} %get-tuple-element.178), channel_id=1, source_target_pairs={{4,0},{8,4},{12,8},{16,12},{20,16},{24,20},{28,24},{0,28},{5,1},{9... | collective-permute-start | bytes 16208 | tf_op jit(solution)/shard_map/ppermute | solution.py:18
  265.6 261.2 %all-reduce.5.cloned.1.call-start = ((), (), s32[]{:S(2)}) async-start(), calls=%async_computation | async-start | bytes 8192000 | tf_op jit(solution)/shard_map/psum | solution.py:100
  278.0 15.3 %collective-permute-start.10 = (bf16[300,3,134]{0,2,1:T(8,128)(2,1)S(1)}, bf16[300,3,134]{0,2,1:T(8,128)(2,1)}, u32[]{:S(2)}, u32[]{:S(2)}) collective-permute-start(bf16[300,3,134]{0,2,1:T(8,128)(2,1)S(1)} %copy.97), channel_id=1, source_target_pairs={{1,0},{2,1},{3,2},{0,3},{5,4},{6,5},{7,6},{4,7},{9,8},{10,9},{11,1... | collective-permute-start | bytes 723608 | tf_op jit(solution)/shard_map/ppermute | solution.py:18
  278.9 16.4 %collective-permute-start.9 = (bf16[300,3,134]{0,2,1:T(8,128)(2,1)S(1)}, bf16[300,3,134]{0,2,1:T(8,128)(2,1)S(1)}, u32[]{:S(2)}, u32[]{:S(2)}) collective-permute-start(bf16[300,3,134]{0,2,1:T(8,128)(2,1)S(1)} %copy.97), channel_id=1, source_target_pairs={{0,1},{1,2},{2,3},{3,0},{4,5},{5,6},{6,7},{7,4},{8,9},{9,10},{10,1... | collective-permute-start | bytes 723608 | tf_op jit(solution)/shard_map/ppermute | solution.py:17
  301.2 16.2 %copy-start.10 = (f32[38,8,3,128]{3,1,2,0:T(8,128)S(1)}, f32[38,8,3,128]{3,1,2,0:T(8,128)}, u32[]{:S(2)}) copy-start(f32[38,8,3,128]{3,1,2,0:T(8,128)} %copy.109) | copy-start | bytes 1400836
  301.2 16.2 %copy-start.22 = (bf16[1200,300]{0,1:T(8,128)(2,1)S(1)}, bf16[1200,300]{0,1:T(8,128)(2,1)}, u32[]{:S(2)}) copy-start(bf16[1200,300]{0,1:T(8,128)(2,1)} %param.21) | copy-start | bytes 2160004
  301.2 16.2 %copy-start.73 = (f32[384]{0:T(512)S(1)}, f32[384]{0:T(512)}, u32[]{:S(2)}) copy-start(f32[384]{0:T(512)} %copy-done.72) | copy-start | bytes 4612
  301.9 14.4 %collective-permute-start.11 = (bf16[300,3,134]{0,2,1:T(8,128)(2,1)S(1)}, bf16[300,3,134]{0,2,1:T(8,128)(2,1)}, u32[]{:S(2)}, u32[]{:S(2)}) collective-permute-start(bf16[300,3,134]{0,2,1:T(8,128)(2,1)S(1)} %copy.101), channel_id=1, source_target_pairs={{0,4},{4,0},{8,12},{12,8},{16,20},{20,16},{24,28},{28,24},{1,5},{5... | collective-permute-start | bytes 723608 | tf_op jit(solution)/shard_map/ppermute | solution.py:24
  316.3 9.7 %collective-permute-start.12 = (bf16[300,3,134]{0,2,1:T(8,128)(2,1)}, bf16[300,3,134]{0,2,1:T(8,128)(2,1)S(1)}, u32[]{:S(2)}, u32[]{:S(2)}) collective-permute-start(bf16[300,3,134]{0,2,1:T(8,128)(2,1)} %collective-permute-done.11), channel_id=1, source_target_pairs={{0,8},{4,12},{8,0},{12,4},{16,24},{20,28},{24,16},{28,20},{1,9},{5... | collective-permute-start | bytes 723608 | tf_op jit(solution)/shard_map/ppermute | solution.py:24
  326.0 42.3 %collective-permute-start.13 = (bf16[300,3,134]{0,2,1:T(8,128)(2,1)S(1)}, bf16[300,3,134]{0,2,1:T(8,128)(2,1)S(1)}, u32[]{:S(2)}, u32[]{:S(2)}) collective-permute-start(bf16[300,3,134]{0,2,1:T(8,128)(2,1)S(1)} %collective-permute-done.12), channel_id=1, source_target_pairs={{0,16},{4,20},{8,24},{12,28},{16,0},{20,4},{24,8},{28,12},{1,17},{... | collective-permute-start | bytes 723608 | tf_op jit(solution)/shard_map/ppermute | solution.py:24
  387.3 14.4 %copy-start.17 = (bf16[300,3,128]{2,0,1:T(8,128)(2,1)S(1)}, bf16[300,3,128]{2,0,1:T(8,128)(2,1)}, u32[]{:S(2)}) copy-start(bf16[300,3,128]{2,0,1:T(8,128)(2,1)} %param.17) | copy-start | bytes 691204
  387.3 14.4 %copy-start.79 = (f32[300]{0:T(512)S(1)}, f32[300]{0:T(512)}, u32[]{:S(2)}) copy-start(f32[300]{0:T(512)} %get-tuple-element.154) | copy-start | bytes 3604
  387.3 14.4 %copy-start.81 = (f32[300]{0:T(512)S(1)}, f32[300]{0:T(512)}, u32[]{:S(2)}) copy-start(f32[300]{0:T(512)} %get-tuple-element.155) | copy-start | bytes 3604
  387.3 14.4 %copy-start.83 = (f32[300]{0:T(512)S(1)}, f32[300]{0:T(512)}, u32[]{:S(2)}) copy-start(f32[300]{0:T(512)} %get-tuple-element.156) | copy-start | bytes 3604
  387.3 14.4 %copy-start.85 = (f32[300]{0:T(512)S(1)}, f32[300]{0:T(512)}, u32[]{:S(2)}) copy-start(f32[300]{0:T(512)} %get-tuple-element.157) | copy-start | bytes 3604
  387.3 14.4 %copy-start.87 = (f32[300]{0:T(512)S(1)}, f32[300]{0:T(512)}, u32[]{:S(2)}) copy-start(f32[300]{0:T(512)} %get-tuple-element.158) | copy-start | bytes 3604
  387.3 14.4 %copy-start.89 = (f32[300]{0:T(512)S(1)}, f32[300]{0:T(512)}, u32[]{:S(2)}) copy-start(f32[300]{0:T(512)} %get-tuple-element.159) | copy-start | bytes 3604
  387.3 14.4 %copy-start.91 = (f32[300]{0:T(512)S(1)}, f32[300]{0:T(512)}, u32[]{:S(2)}) copy-start(f32[300]{0:T(512)} %get-tuple-element.160) | copy-start | bytes 3604
  387.3 14.4 %copy-start.93 = (f32[300]{0:T(512)S(1)}, f32[300]{0:T(512)}, u32[]{:S(2)}) copy-start(f32[300]{0:T(512)} %get-tuple-element.161) | copy-start | bytes 3604
  387.3 14.4 %copy-start.95 = (f32[300]{0:T(512)S(1)}, f32[300]{0:T(512)}, u32[]{:S(2)}) copy-start(f32[300]{0:T(512)} %get-tuple-element.162) | copy-start | bytes 3604
  387.4 14.4 %copy-start.97 = (f32[300]{0:T(512)S(1)}, f32[300]{0:T(512)}, u32[]{:S(2)}) copy-start(f32[300]{0:T(512)} %get-tuple-element.163) | copy-start | bytes 3604
  387.4 14.4 %copy-start.99 = (f32[300]{0:T(512)S(1)}, f32[300]{0:T(512)}, u32[]{:S(2)}) copy-start(f32[300]{0:T(512)} %get-tuple-element.164) | copy-start | bytes 3604
  387.4 14.4 %copy-start.101 = (f32[300]{0:T(512)S(1)}, f32[300]{0:T(512)}, u32[]{:S(2)}) copy-start(f32[300]{0:T(512)} %get-tuple-element.135) | copy-start | bytes 3604
  387.4 14.4 %copy-start.103 = (f32[300]{0:T(512)S(1)}, f32[300]{0:T(512)}, u32[]{:S(2)}) copy-start(f32[300]{0:T(512)} %get-tuple-element.139) | copy-start | bytes 3604
  387.4 14.4 %copy-start.105 = (f32[300]{0:T(512)S(1)}, f32[300]{0:T(512)}, u32[]{:S(2)}) copy-start(f32[300]{0:T(512)} %get-tuple-element.140) | copy-start | bytes 3604
  387.4 14.4 %copy-start.107 = (f32[300]{0:T(512)S(1)}, f32[300]{0:T(512)}, u32[]{:S(2)}) copy-start(f32[300]{0:T(512)} %get-tuple-element.141) | copy-start | bytes 3604
  387.4 14.4 %copy-start.109 = (f32[300]{0:T(512)S(1)}, f32[300]{0:T(512)}, u32[]{:S(2)}) copy-start(f32[300]{0:T(512)} %get-tuple-element.142) | copy-start | bytes 3604
  387.4 14.4 %copy-start.111 = (f32[300]{0:T(512)S(1)}, f32[300]{0:T(512)}, u32[]{:S(2)}) copy-start(f32[300]{0:T(512)} %get-tuple-element.143) | copy-start | bytes 3604
  387.4 14.4 %copy-start.113 = (f32[300]{0:T(512)S(1)}, f32[300]{0:T(512)}, u32[]{:S(2)}) copy-start(f32[300]{0:T(512)} %get-tuple-element.144) | copy-start | bytes 3604
  (97 other events, 451.4 us)
Sparse Core Ops, SparseCore 0:
  265.7 90.8 all-reduce.6
  372.7 154.0 all-reduce.4
